TPU v7x, 256 devices: a whole 4x4x8 slice. The times are simulated.
256 devices in a mesh: row: 16 (over y, z_lo, core), col: 16 (over z_hi, x).
Axes of the slice: x: 4, y: 4, z: 8 (z_hi: 4, z_lo: 2; z = z_hi * 2 + z_lo), core: 2. Of those that a mesh axis runs over, the one named last changes fastest.
Arguments:
- features: bfloat16 [131072, 256], P(('row', 'col')), may hold values from -6 to 6
- w_self: bfloat16 [256, 256], replicated, may hold values from -0.375 to 0.375
- w_neigh: bfloat16 [256, 256], replicated, may hold values from -3 to 3
- cotangent: bfloat16 [131072, 256], P(('row', 'col')), may hold values from -6 to 6
- degree: int32 [131072], P(('row', 'col')), may hold values from 64 to 256
- tile_rows: int32 [65536], P(('row', 'col')), may hold values from 0 to 63
- tile_cols: int32 [65536], P(('row', 'col')), may hold values from 0 to 63
- tile_edges: int32 [4, 65536, 128], P(None, ('row', 'col')), may hold values from 0 to 127
- tile_count: int32 [256], P(('row', 'col')), may hold values from 4 to 256, as said below
Outputs:
- activations: bfloat16 [131072, 256], P(('row', 'col'))
- feature_grad: bfloat16 [131072, 256], P(('row', 'col'))
- grad_self: float32 [256, 256], replicated
- grad_neigh: float32 [256, 256], replicated
Inputs may be any that keep to these rules, and one draw needn't show every extreme that they name: The busiest device uses all 256 of its slots; slots from tile_count on are ignored.
All inputs are finite; a program needn't handle non-finite values.
Results may differ from a plain program's by a relative error of at most 0.0059.
Values may be sent and summed in bfloat16 or wider, within the bound.
No kernel may reach another device: no remote copies, remote signals or barrier semaphores. Data moves between devices by JAX's collectives and lax.ppermute only.
A program may use at most 64 MiB of HBM per device.

v0:
```python
import math
import jax
import jax.numpy as jnp
from jax import lax
from jax.sharding import PartitionSpec as P


def tile_masks(edges_here, use_here):
    tile_size = edges_here.shape[2]
    matches = edges_here[:, :, :, None] == jnp.arange(tile_size, dtype=jnp.int32)
    multiplicity = jnp.sum(matches.astype(jnp.float32), axis=0)
    return (multiplicity * use_here[:, None, None]).astype(jnp.bfloat16)


def sum_weights(part_self, part_neigh):
    return lax.psum((part_self, part_neigh), ("row", "col"))


def spread_back(dscaled, row_blocks, col_blocks, edge_blocks, use_blocks, col_tile_count):
    tile_size = edge_blocks.shape[3]
    feature_dim = dscaled.shape[1]
    row_nodes = lax.all_gather(dscaled, "col", axis=0, tiled=True)
    row_tiles = row_nodes.reshape(-1, tile_size, feature_dim)

    def backward_round(running, inputs):
        rows_here, cols_here, edges_here, use_here = inputs
        pattern = tile_masks(edges_here, use_here)
        contribution = jnp.einsum(
            "bqc,bqf->bcf", pattern, row_tiles[rows_here], preferred_element_type=jnp.float32
        )
        return (running.at[cols_here].add(contribution), None)

    start_value = jnp.zeros((col_tile_count, tile_size, feature_dim), jnp.float32)
    partial_grads, _ = lax.scan(
        backward_round, start_value, (row_blocks, col_blocks, edge_blocks, use_blocks)
    )
    return lax.psum_scatter(
        partial_grads.reshape(-1, feature_dim), "row", scatter_dimension=0, tiled=True
    )


def per_device(
    features, w_self, w_neigh, cotangent, degree, tile_rows, tile_cols, tile_edges, tile_count
):
    local_rows, feature_dim = features.shape
    tile_size = tile_edges.shape[2]
    slot_count = tile_rows.shape[0]
    row_devices = lax.axis_size("row")
    col_devices = lax.axis_size("col")
    in_use = (jnp.arange(slot_count, dtype=jnp.int32) < tile_count[0]).astype(jnp.float32)
    block_size = math.gcd(slot_count, 32)
    rounds = slot_count // block_size
    edge_blocks = tile_edges.reshape(tile_edges.shape[0], rounds, block_size, tile_size).transpose(
        1, 0, 2, 3
    )
    row_blocks = tile_rows.reshape(rounds, block_size)
    col_blocks = tile_cols.reshape(rounds, block_size)
    use_blocks = in_use.reshape(rounds, block_size)
    row_tile_count = local_rows * col_devices // tile_size
    col_tile_count = local_rows * row_devices // tile_size
    column_nodes = lax.all_gather(features, "row", axis=0, tiled=True)
    column_tiles = column_nodes.reshape(-1, tile_size, feature_dim)

    def forward_round(running, inputs):
        rows_here, cols_here, edges_here, use_here = inputs
        pattern = tile_masks(edges_here, use_here)
        product = jnp.einsum(
            "bqc,bcf->bqf", pattern, column_tiles[cols_here], preferred_element_type=jnp.float32
        )
        return (running.at[rows_here].add(product), None)

    start_value = jnp.zeros((row_tile_count, tile_size, feature_dim), jnp.float32)
    partial_sums, _ = lax.scan(
        forward_round, start_value, (row_blocks, col_blocks, edge_blocks, use_blocks)
    )
    neighbour_sum = lax.psum_scatter(
        partial_sums.reshape(-1, feature_dim), "col", scatter_dimension=0, tiled=True
    )
    degree_wide = degree.astype(jnp.float32)[:, None]
    aggregate = (neighbour_sum / degree_wide).astype(jnp.bfloat16)
    preact = jnp.dot(features, w_self, preferred_element_type=jnp.float32) + jnp.dot(
        aggregate, w_neigh, preferred_element_type=jnp.float32
    )
    sigmoid_pre = jax.nn.sigmoid(preact)
    activations = (preact * sigmoid_pre).astype(jnp.bfloat16)
    slope = sigmoid_pre * (1.0 + preact * (1.0 - sigmoid_pre))
    dpreact = (cotangent.astype(jnp.float32) * slope).astype(jnp.bfloat16)
    part_self = jnp.einsum("nf,ng->fg", features, dpreact, preferred_element_type=jnp.float32)
    part_neigh = jnp.einsum("nf,ng->fg", aggregate, dpreact, preferred_element_type=jnp.float32)
    dscaled = (
        jnp.einsum("ng,fg->nf", dpreact, w_neigh, preferred_element_type=jnp.float32) / degree_wide
    ).astype(jnp.bfloat16)
    neighbour_grad = spread_back(
        dscaled, row_blocks, col_blocks, edge_blocks, use_blocks, col_tile_count
    )
    grad_pair = sum_weights(part_self, part_neigh)
    own_grad = jnp.einsum("ng,fg->nf", dpreact, w_self, preferred_element_type=jnp.float32)
    feature_grad = (own_grad + neighbour_grad).astype(jnp.bfloat16)
    total_nodes = local_rows * row_devices * col_devices
    grad_scale = 1.0 / math.sqrt(total_nodes)
    return (activations, feature_grad, grad_pair[0] * grad_scale, grad_pair[1] * grad_scale)


def solution(mesh):
    return jax.shard_map(
        per_device,
        mesh=mesh,
        in_specs=(
            P(("row", "col"), None),
            P(),
            P(),
            P(("row", "col"), None),
            P(("row", "col")),
            P(("row", "col")),
            P(("row", "col")),
            P(None, ("row", "col"), None),
            P(("row", "col")),
        ),
        out_specs=(P(("row", "col"), None), P(("row", "col"), None), P(), P()),
        check_vma=False,
    )
```

profile of v0, /device:TPU:2, one launch (start us, length us, event | category | flops | bytes accessed | tf_op | source)
XLA Modules:
  0.0 771.7 jit_solution(11886097251280555593)
XLA Ops:
  11.2 41.7 %all-gather.3.cloned.1.call-done = bf16[8192,256]{1,0:T(8,128)(2,1)} async-done(((bf16[512,256]{1,0:T(8,128)(2,1)}), bf16[8192,256]{1,0:T(8,128)(2,1)}) %all-gather.3.cloned.1.call-update) | async-done | bytes 4194320 | tf_op jit(solution)/shard_map/all_gather | solution.py:61
  52.9 4.3 broadcast.81.clone
  57.1 147.1 %while.20 = (s32[]{:T(128)}, f32[64,128,256]{2,1,0:T(8,128)}, s32[8,32]{1,0:T(8,128)S(1)}, s32[8,4,32,128]{3,2,1,0:T(8,128)S(1)}, f32[8,32]{1,0:T(8,128)S(1)}, /...) while((s32[]{:T(128)}, f32[64,128,256]{2,1,0:T(8,128)}, s32[8,32]{1,0:T(8,128)S(1)}, ...), condition=%wide.region_3.4_spmd, body=%wide.region_0.3_spmd.sunk | while | flops 276300992 | bytes 27465064 | solution.py:73
  65.7 9.8 %scatter_fusion = f32[64,128,256]{2,1,0:T(8,128)} fusion(f32[64,128,256]{2,1,0:T(8,128)} %get-tuple-element.261, s32[32]{0:T(128)S(1)} %get-tuple-element.241, f32[32,128,256]{2,1,0:T(8,128)} %fusion.44), kind=kCustom, calls=%fused_computation.2.clone.1 | custom fusion | flops 1048576 | bytes 12583040 | tf_op jit(solution)/shard_map/while/body/eval_jaxpr/scatter-add | solution.py:70
  84.2 9.7 %scatter_fusion = f32[64,128,256]{2,1,0:T(8,128)} fusion(f32[64,128,256]{2,1,0:T(8,128)} %get-tuple-element.261, s32[32]{0:T(128)S(1)} %get-tuple-element.241, f32[32,128,256]{2,1,0:T(8,128)} %fusion.44), kind=kCustom, calls=%fused_computation.2.clone.1 | custom fusion | flops 1048576 | bytes 12583040 | tf_op jit(solution)/shard_map/while/body/eval_jaxpr/scatter-add | solution.py:70
  102.4 9.7 %scatter_fusion = f32[64,128,256]{2,1,0:T(8,128)} fusion(f32[64,128,256]{2,1,0:T(8,128)} %get-tuple-element.261, s32[32]{0:T(128)S(1)} %get-tuple-element.241, f32[32,128,256]{2,1,0:T(8,128)} %fusion.44), kind=kCustom, calls=%fused_computation.2.clone.1 | custom fusion | flops 1048576 | bytes 12583040 | tf_op jit(solution)/shard_map/while/body/eval_jaxpr/scatter-add | solution.py:70
  120.7 9.6 %scatter_fusion = f32[64,128,256]{2,1,0:T(8,128)} fusion(f32[64,128,256]{2,1,0:T(8,128)} %get-tuple-element.261, s32[32]{0:T(128)S(1)} %get-tuple-element.241, f32[32,128,256]{2,1,0:T(8,128)} %fusion.44), kind=kCustom, calls=%fused_computation.2.clone.1 | custom fusion | flops 1048576 | bytes 12583040 | tf_op jit(solution)/shard_map/while/body/eval_jaxpr/scatter-add | solution.py:70
  139.0 9.8 %scatter_fusion = f32[64,128,256]{2,1,0:T(8,128)} fusion(f32[64,128,256]{2,1,0:T(8,128)} %get-tuple-element.261, s32[32]{0:T(128)S(1)} %get-tuple-element.241, f32[32,128,256]{2,1,0:T(8,128)} %fusion.44), kind=kCustom, calls=%fused_computation.2.clone.1 | custom fusion | flops 1048576 | bytes 12583040 | tf_op jit(solution)/shard_map/while/body/eval_jaxpr/scatter-add | solution.py:70
  157.3 9.8 %scatter_fusion = f32[64,128,256]{2,1,0:T(8,128)} fusion(f32[64,128,256]{2,1,0:T(8,128)} %get-tuple-element.261, s32[32]{0:T(128)S(1)} %get-tuple-element.241, f32[32,128,256]{2,1,0:T(8,128)} %fusion.44), kind=kCustom, calls=%fused_computation.2.clone.1 | custom fusion | flops 1048576 | bytes 12583040 | tf_op jit(solution)/shard_map/while/body/eval_jaxpr/scatter-add | solution.py:70
  175.7 9.9 %scatter_fusion = f32[64,128,256]{2,1,0:T(8,128)} fusion(f32[64,128,256]{2,1,0:T(8,128)} %get-tuple-element.261, s32[32]{0:T(128)S(1)} %get-tuple-element.241, f32[32,128,256]{2,1,0:T(8,128)} %fusion.44), kind=kCustom, calls=%fused_computation.2.clone.1 | custom fusion | flops 1048576 | bytes 12583040 | tf_op jit(solution)/shard_map/while/body/eval_jaxpr/scatter-add | solution.py:70
  194.2 10.0 %scatter_fusion = f32[64,128,256]{2,1,0:T(8,128)} fusion(f32[64,128,256]{2,1,0:T(8,128)} %get-tuple-element.261, s32[32]{0:T(128)S(1)} %get-tuple-element.241, f32[32,128,256]{2,1,0:T(8,128)} %fusion.44), kind=kCustom, calls=%fused_computation.2.clone.1 | custom fusion | flops 1048576 | bytes 12583040 | tf_op jit(solution)/shard_map/while/body/eval_jaxpr/scatter-add | solution.py:70
  205.4 119.9 %reduce-scatter.3.cloned.1.call-done = f32[512,256]{1,0:T(8,128)} async-done(((f32[8192,256]{1,0:T(8,128)}), f32[512,256]{1,0:T(8,128)}) %reduce-scatter.3.cloned.1.call-update) | async-done | bytes 524304 | tf_op jit(solution)/shard_map/reduce_scatter | solution.py:76
  330.7 72.7 %all-gather.5.cloned.1.call-done = bf16[8192,256]{1,0:T(8,128)(2,1)} async-done(((bf16[512,256]{1,0:T(8,128)(2,1)}), bf16[8192,256]{1,0:T(8,128)(2,1)}) %all-gather.5.cloned.1.call-update) | async-done | bytes 4194320 | tf_op jit(solution)/shard_map/all_gather | solution.py:22
  407.6 150.2 %while.21 = (s32[]{:T(128)}, f32[64,128,256]{2,1,0:T(8,128)}, s32[8,32]{1,0:T(8,128)S(1)}, s32[8,4,32,128]{3,2,1,0:T(8,128)S(1)}, f32[8,32]{1,0:T(8,128)S(1)}, /...) while((s32[]{:T(128)}, f32[64,128,256]{2,1,0:T(8,128)}, s32[8,32]{1,0:T(8,128)S(1)}, ...), condition=%wide.region_8.9_spmd, body=%wide.region_5.8_spmd.sunk | while | flops 276300992 | bytes 27465064 | solution.py:34
  416.4 9.9 %scatter_fusion.1 = f32[64,128,256]{2,1,0:T(8,128)} fusion(f32[64,128,256]{2,1,0:T(8,128)} %get-tuple-element.285, s32[32]{0:T(128)S(1)} %get-tuple-element.250, f32[32,128,256]{2,1,0:T(8,128)} %fusion.48), kind=kCustom, calls=%fused_computation.3.clone.1 | custom fusion | flops 1048576 | bytes 12583040 | tf_op jit(solution)/shard_map/while/body/eval_jaxpr/scatter-add | solution.py:31
  435.1 10.1 %scatter_fusion.1 = f32[64,128,256]{2,1,0:T(8,128)} fusion(f32[64,128,256]{2,1,0:T(8,128)} %get-tuple-element.285, s32[32]{0:T(128)S(1)} %get-tuple-element.250, f32[32,128,256]{2,1,0:T(8,128)} %fusion.48), kind=kCustom, calls=%fused_computation.3.clone.1 | custom fusion | flops 1048576 | bytes 12583040 | tf_op jit(solution)/shard_map/while/body/eval_jaxpr/scatter-add | solution.py:31
  453.9 10.0 %scatter_fusion.1 = f32[64,128,256]{2,1,0:T(8,128)} fusion(f32[64,128,256]{2,1,0:T(8,128)} %get-tuple-element.285, s32[32]{0:T(128)S(1)} %get-tuple-element.250, f32[32,128,256]{2,1,0:T(8,128)} %fusion.48), kind=kCustom, calls=%fused_computation.3.clone.1 | custom fusion | flops 1048576 | bytes 12583040 | tf_op jit(solution)/shard_map/while/body/eval_jaxpr/scatter-add | solution.py:31
  472.7 10.0 %scatter_fusion.1 = f32[64,128,256]{2,1,0:T(8,128)} fusion(f32[64,128,256]{2,1,0:T(8,128)} %get-tuple-element.285, s32[32]{0:T(128)S(1)} %get-tuple-element.250, f32[32,128,256]{2,1,0:T(8,128)} %fusion.48), kind=kCustom, calls=%fused_computation.3.clone.1 | custom fusion | flops 1048576 | bytes 12583040 | tf_op jit(solution)/shard_map/while/body/eval_jaxpr/scatter-add | solution.py:31
  491.5 10.1 %scatter_fusion.1 = f32[64,128,256]{2,1,0:T(8,128)} fusion(f32[64,128,256]{2,1,0:T(8,128)} %get-tuple-element.285, s32[32]{0:T(128)S(1)} %get-tuple-element.250, f32[32,128,256]{2,1,0:T(8,128)} %fusion.48), kind=kCustom, calls=%fused_computation.3.clone.1 | custom fusion | flops 1048576 | bytes 12583040 | tf_op jit(solution)/shard_map/while/body/eval_jaxpr/scatter-add | solution.py:31
  510.4 10.1 %scatter_fusion.1 = f32[64,128,256]{2,1,0:T(8,128)} fusion(f32[64,128,256]{2,1,0:T(8,128)} %get-tuple-element.285, s32[32]{0:T(128)S(1)} %get-tuple-element.250, f32[32,128,256]{2,1,0:T(8,128)} %fusion.48), kind=kCustom, calls=%fused_computation.3.clone.1 | custom fusion | flops 1048576 | bytes 12583040 | tf_op jit(solution)/shard_map/while/body/eval_jaxpr/scatter-add | solution.py:31
  529.2 9.9 %scatter_fusion.1 = f32[64,128,256]{2,1,0:T(8,128)} fusion(f32[64,128,256]{2,1,0:T(8,128)} %get-tuple-element.285, s32[32]{0:T(128)S(1)} %get-tuple-element.250, f32[32,128,256]{2,1,0:T(8,128)} %fusion.48), kind=kCustom, calls=%fused_computation.3.clone.1 | custom fusion | flops 1048576 | bytes 12583040 | tf_op jit(solution)/shard_map/while/body/eval_jaxpr/scatter-add | solution.py:31
  547.9 10.0 %scatter_fusion.1 = f32[64,128,256]{2,1,0:T(8,128)} fusion(f32[64,128,256]{2,1,0:T(8,128)} %get-tuple-element.285, s32[32]{0:T(128)S(1)} %get-tuple-element.250, f32[32,128,256]{2,1,0:T(8,128)} %fusion.48), kind=kCustom, calls=%fused_computation.3.clone.1 | custom fusion | flops 1048576 | bytes 12583040 | tf_op jit(solution)/shard_map/while/body/eval_jaxpr/scatter-add | solution.py:31
  557.9 103.7 %all-reduce.3.cloned.1.call-done = (f32[256,256]{0,1:T(8,128)}, f32[256,256]{0,1:T(8,128)}) async-done(((f32[256,256]{0,1:T(8,128)}, f32[256,256]{0,1:T(8,128)}), (f32[256,256]{0,1:T(8,128)}, f32[256,256]{0,1:T(8,128)})) %all-reduce.3.cloned.1.call-update) | async-done | bytes 524304 | tf_op jit(solution)/shard_map/psum | solution.py:16
  664.4 98.7 %reduce-scatter.5.cloned.1.call-done = f32[512,256]{1,0:T(8,128)} async-done(((f32[8192,256]{1,0:T(8,128)}), f32[512,256]{1,0:T(8,128)}) %reduce-scatter.5.cloned.1.call-update) | async-done | bytes 524304 | tf_op jit(solution)/shard_map/reduce_scatter | solution.py:37
  (148 shorter events, 157.3 us)
Async XLA Ops:
  7.2 319.3 %copy-start = (bf16[256,256]{1,0:T(8,128)(2,1)S(1)}, bf16[256,256]{1,0:T(8,128)(2,1)}, u32[]{:S(2)}) copy-start(bf16[256,256]{1,0:T(8,128)(2,1)} %param.15) | copy-start | bytes 393220
  7.2 45.7 %all-gather.3.cloned.1.call-start = ((), (), s32[]{:S(2)}) async-start(), calls=%async_computation.2 | async-start | bytes 4456448 | tf_op jit(solution)/shard_map/all_gather | solution.py:61
  7.9 317.4 %reduce-scatter.3.cloned.1.call-start = ((), (), s32[]{:S(2)}) async-start(), calls=%async_computation.3 | async-start | bytes 8912896 | tf_op jit(solution)/shard_map/reduce_scatter | solution.py:76
  204.2 0.7 copy-start.3
  204.2 1.0 copy-start.1
  204.2 1.0 copy-start.2
  204.2 122.3 %copy-start.4 = (bf16[512,256]{1,0:T(8,128)(2,1)S(1)}, bf16[512,256]{1,0:T(8,128)(2,1)}, u32[]{:S(2)}) copy-start(bf16[512,256]{1,0:T(8,128)(2,1)} %param.16) | copy-start | bytes 786436
  204.2 199.1 %all-gather.5.cloned.1.call-start = ((), (), s32[]{:S(2)}) async-start(), calls=%async_computation.4 | async-start | bytes 4456448 | tf_op jit(solution)/shard_map/all_gather | solution.py:22
  328.6 333.0 %all-reduce.3.cloned.1.call-start = ((), (), s32[]{:S(2)}) async-start(), calls=%async_computation.6 | async-start | bytes 1048576 | tf_op jit(solution)/shard_map/psum | solution.py:16
  330.6 432.5 %reduce-scatter.5.cloned.1.call-start = ((), (), s32[]{:S(2)}) async-start(), calls=%async_computation.5 | async-start | bytes 8912896 | tf_op jit(solution)/shard_map/reduce_scatter | solution.py:37
Sparse Core Ops, SparseCore 0:
  9.9 42.9 all-gather.2
  204.4 120.8 reduce-scatter.2
  328.7 74.6 all-gather.4
  409.4 252.1 all-reduce.2
  664.0 99.0 reduce-scatter.4
where the time goes:
time: 773 us; the launch traced here: 772 us
  waiting for transfers between devices  437 us (57%)
  other arithmetic  208 us (27%)
  local copies, waits for them, and re-layouts  60 us (8%)
  matrix products  51.1 us (7%)
  between operations  14.5 us (2%)
    reduce_scatter x1, waiting for transfers between devices, per_device(): lax.psum_scatter(partial_sums.reshape(-1, feature_dim), 'col', scatter_di...  120 us
    psum x1, waiting for transfers between devices, sum_weights(): return lax.psum((part_self, part_neigh), ('row', 'col'))  104 us
    reduce_scatter x1, waiting for transfers between devices, spread_back(): lax.psum_scatter(partial_grads.reshape(-1, feature_dim), 'row', scatter_d...  98.7 us
    scatter-add x8, other arithmetic, backward_round(): return (running.at[cols_here].add(contribution), None)  80.1 us
    scatter-add x8, other arithmetic, forward_round(): return (running.at[rows_here].add(product), None)  78.3 us
    all_gather x1, waiting for transfers between devices, spread_back(): row_nodes = lax.all_gather(dscaled, 'col', axis=0, tiled=True)  72.7 us
    reduce_sum x16, other arithmetic, tile_masks(): multiplicity = jnp.sum(matches.astype(jnp.float32), axis=0)  46.9 us
    all_gather x1, waiting for transfers between devices, per_device(): column_nodes = lax.all_gather(features, 'row', axis=0, tiled=True)  41.7 us
  transfers between devices with their start and end apart: 5, of which 5 were waited for; matrix products, arithmetic and copies ran while one was open for 21% of the time, Pallas kernels for 0%

commit v1 on v0

--- a/solution.py
+++ b/solution.py
@@ -1,8 +1,18 @@
+import functools
 import math
 import jax
 import jax.numpy as jnp
 from jax import lax
 from jax.sharding import PartitionSpec as P
+from jax.lax import psum
+
+
+def change_widths(matrix, lane_axis, named_axis):
+    left_arr = psum(matrix, axis_name=lane_axis)
+    return psum(left_arr, axis_name=named_axis)
+
+
+_process_spans = functools.partial(change_widths, lane_axis="col", named_axis="row")
 
 
 def tile_masks(edges_here, use_here):
@@ -13,7 +23,7 @@
 
 
 def sum_weights(part_self, part_neigh):
-    return lax.psum((part_self, part_neigh), ("row", "col"))
+    return _process_spans((part_self, part_neigh))
 
 
 def spread_back(dscaled, row_blocks, col_blocks, edge_blocks, use_blocks, col_tile_count):

time: 773 us -> 837 us (1.083)
  waiting for transfers between devices: 437 us -> 502 us
    psum x1 -> x2, waiting for transfers between devices: 104 us -> 164 us  [the longest x1 164 us: change_widths(): left_arr = psum(matrix, axis_name=lane_axis)]
  transfers between devices with their start and end apart: 5 -> 6, of which waited for: 5 -> 5; matrix products, arithmetic and copies ran while one was open for 21% -> 19% of each run, Pallas kernels for 0% -> 0%
where the time goes in v1:
time: 837 us; the launch traced here: 836 us
  waiting for transfers between devices  502 us (60%)
  other arithmetic  208 us (25%)
  local copies, waits for them, and re-layouts  60 us (7%)
  matrix products  51 us (6%)
  between operations  14.8 us (2%)
    psum x1, waiting for transfers between devices, change_widths(): left_arr = psum(matrix, axis_name=lane_axis)  164 us
    reduce_scatter x1, waiting for transfers between devices, per_device(): lax.psum_scatter(partial_sums.reshape(-1, feature_dim), 'col', scatter_di...  120 us
    reduce_scatter x1, waiting for transfers between devices, spread_back(): lax.psum_scatter(partial_grads.reshape(-1, feature_dim), 'row', scatter_d...  97.6 us
    scatter-add x8, other arithmetic, backward_round(): return (running.at[cols_here].add(contribution), None)  80.1 us
    scatter-add x8, other arithmetic, forward_round(): return (running.at[rows_here].add(product), None)  78.2 us
    all_gather x1, waiting for transfers between devices, spread_back(): row_nodes = lax.all_gather(dscaled, 'col', axis=0, tiled=True)  78 us
    reduce_sum x16, other arithmetic, tile_masks(): multiplicity = jnp.sum(matches.astype(jnp.float32), axis=0)  46.9 us
    all_gather x1, waiting for transfers between devices, per_device(): column_nodes = lax.all_gather(features, 'row', axis=0, tiled=True)  41.7 us
  transfers between devices with their start and end apart: 6, of which 5 were waited for; matrix products, arithmetic and copies ran while one was open for 19% of the time, Pallas kernels for 0%

profile of v1, /device:TPU:2, one launch (start us, length us, event | category | flops | bytes accessed | tf_op | source)
XLA Modules:
  0.0 835.8 jit_solution(13679926930401774520)
XLA Ops:
  11.2 41.7 %all-gather.3.cloned.1.call-done = bf16[8192,256]{1,0:T(8,128)(2,1)} async-done(((bf16[512,256]{1,0:T(8,128)(2,1)}), bf16[8192,256]{1,0:T(8,128)(2,1)}) %all-gather.3.cloned.1.call-update) | async-done | bytes 4194320 | tf_op jit(solution)/shard_map/all_gather | solution.py:71
  52.9 4.3 broadcast.81.clone
  57.1 146.8 %while.20 = (s32[]{:T(128)}, f32[64,128,256]{2,1,0:T(8,128)}, s32[8,32]{1,0:T(8,128)S(1)}, s32[8,4,32,128]{3,2,1,0:T(8,128)S(1)}, f32[8,32]{1,0:T(8,128)S(1)}, /...) while((s32[]{:T(128)}, f32[64,128,256]{2,1,0:T(8,128)}, s32[8,32]{1,0:T(8,128)S(1)}, ...), condition=%wide.region_3.4_spmd, body=%wide.region_0.3_spmd.sunk | while | flops 276300992 | bytes 27465064 | solution.py:83
  65.7 9.8 %scatter_fusion = f32[64,128,256]{2,1,0:T(8,128)} fusion(f32[64,128,256]{2,1,0:T(8,128)} %get-tuple-element.263, s32[32]{0:T(128)S(1)} %get-tuple-element.243, f32[32,128,256]{2,1,0:T(8,128)} %fusion.44), kind=kCustom, calls=%fused_computation.2.clone.1 | custom fusion | flops 1048576 | bytes 12583040 | tf_op jit(solution)/shard_map/while/body/eval_jaxpr/scatter-add | solution.py:80
  84.1 9.7 %scatter_fusion = f32[64,128,256]{2,1,0:T(8,128)} fusion(f32[64,128,256]{2,1,0:T(8,128)} %get-tuple-element.263, s32[32]{0:T(128)S(1)} %get-tuple-element.243, f32[32,128,256]{2,1,0:T(8,128)} %fusion.44), kind=kCustom, calls=%fused_computation.2.clone.1 | custom fusion | flops 1048576 | bytes 12583040 | tf_op jit(solution)/shard_map/while/body/eval_jaxpr/scatter-add | solution.py:80
  102.4 9.7 %scatter_fusion = f32[64,128,256]{2,1,0:T(8,128)} fusion(f32[64,128,256]{2,1,0:T(8,128)} %get-tuple-element.263, s32[32]{0:T(128)S(1)} %get-tuple-element.243, f32[32,128,256]{2,1,0:T(8,128)} %fusion.44), kind=kCustom, calls=%fused_computation.2.clone.1 | custom fusion | flops 1048576 | bytes 12583040 | tf_op jit(solution)/shard_map/while/body/eval_jaxpr/scatter-add | solution.py:80
  120.7 9.7 %scatter_fusion = f32[64,128,256]{2,1,0:T(8,128)} fusion(f32[64,128,256]{2,1,0:T(8,128)} %get-tuple-element.263, s32[32]{0:T(128)S(1)} %get-tuple-element.243, f32[32,128,256]{2,1,0:T(8,128)} %fusion.44), kind=kCustom, calls=%fused_computation.2.clone.1 | custom fusion | flops 1048576 | bytes 12583040 | tf_op jit(solution)/shard_map/while/body/eval_jaxpr/scatter-add | solution.py:80
  139.0 9.7 %scatter_fusion = f32[64,128,256]{2,1,0:T(8,128)} fusion(f32[64,128,256]{2,1,0:T(8,128)} %get-tuple-element.263, s32[32]{0:T(128)S(1)} %get-tuple-element.243, f32[32,128,256]{2,1,0:T(8,128)} %fusion.44), kind=kCustom, calls=%fused_computation.2.clone.1 | custom fusion | flops 1048576 | bytes 12583040 | tf_op jit(solution)/shard_map/while/body/eval_jaxpr/scatter-add | solution.py:80
  157.2 9.8 %scatter_fusion = f32[64,128,256]{2,1,0:T(8,128)} fusion(f32[64,128,256]{2,1,0:T(8,128)} %get-tuple-element.263, s32[32]{0:T(128)S(1)} %get-tuple-element.243, f32[32,128,256]{2,1,0:T(8,128)} %fusion.44), kind=kCustom, calls=%fused_computation.2.clone.1 | custom fusion | flops 1048576 | bytes 12583040 | tf_op jit(solution)/shard_map/while/body/eval_jaxpr/scatter-add | solution.py:80
  175.6 9.8 %scatter_fusion = f32[64,128,256]{2,1,0:T(8,128)} fusion(f32[64,128,256]{2,1,0:T(8,128)} %get-tuple-element.263, s32[32]{0:T(128)S(1)} %get-tuple-element.243, f32[32,128,256]{2,1,0:T(8,128)} %fusion.44), kind=kCustom, calls=%fused_computation.2.clone.1 | custom fusion | flops 1048576 | bytes 12583040 | tf_op jit(solution)/shard_map/while/body/eval_jaxpr/scatter-add | solution.py:80
  194.0 10.0 %scatter_fusion = f32[64,128,256]{2,1,0:T(8,128)} fusion(f32[64,128,256]{2,1,0:T(8,128)} %get-tuple-element.263, s32[32]{0:T(128)S(1)} %get-tuple-element.243, f32[32,128,256]{2,1,0:T(8,128)} %fusion.44), kind=kCustom, calls=%fused_computation.2.clone.1 | custom fusion | flops 1048576 | bytes 12583040 | tf_op jit(solution)/shard_map/while/body/eval_jaxpr/scatter-add | solution.py:80
  205.2 119.9 %reduce-scatter.3.cloned.1.call-done = f32[512,256]{1,0:T(8,128)} async-done(((f32[8192,256]{1,0:T(8,128)}), f32[512,256]{1,0:T(8,128)}) %reduce-scatter.3.cloned.1.call-update) | async-done | bytes 524304 | tf_op jit(solution)/shard_map/reduce_scatter | solution.py:86
  330.5 163.5 %all-reduce.5.cloned.1.call-done = (f32[256,256]{0,1:T(8,128)}, f32[256,256]{0,1:T(8,128)}) async-done(((f32[256,256]{0,1:T(8,128)}, f32[256,256]{0,1:T(8,128)}), (f32[256,256]{0,1:T(8,128)}, f32[256,256]{0,1:T(8,128)})) %all-reduce.5.cloned.1.call-update) | async-done | bytes 524304 | tf_op jit(solution)/shard_map/psum | solution.py:11
  494.1 78.0 %all-gather.5.cloned.1.call-done = bf16[8192,256]{1,0:T(8,128)(2,1)} async-done(((bf16[512,256]{1,0:T(8,128)(2,1)}), bf16[8192,256]{1,0:T(8,128)(2,1)}) %all-gather.5.cloned.1.call-update) | async-done | bytes 4194320 | tf_op jit(solution)/shard_map/all_gather | solution.py:32
  576.4 150.1 %while.21 = (s32[]{:T(128)}, f32[64,128,256]{2,1,0:T(8,128)}, s32[8,32]{1,0:T(8,128)S(1)}, s32[8,4,32,128]{3,2,1,0:T(8,128)S(1)}, f32[8,32]{1,0:T(8,128)S(1)}, /...) while((s32[]{:T(128)}, f32[64,128,256]{2,1,0:T(8,128)}, s32[8,32]{1,0:T(8,128)S(1)}, ...), condition=%wide.region_8.9_spmd, body=%wide.region_5.8_spmd.sunk | while | flops 276300992 | bytes 27465064 | solution.py:44
  585.1 9.9 %scatter_fusion.1 = f32[64,128,256]{2,1,0:T(8,128)} fusion(f32[64,128,256]{2,1,0:T(8,128)} %get-tuple-element.287, s32[32]{0:T(128)S(1)} %get-tuple-element.252, f32[32,128,256]{2,1,0:T(8,128)} %fusion.48), kind=kCustom, calls=%fused_computation.3.clone.1 | custom fusion | flops 1048576 | bytes 12583040 | tf_op jit(solution)/shard_map/while/body/eval_jaxpr/scatter-add | solution.py:41
  603.8 10.1 %scatter_fusion.1 = f32[64,128,256]{2,1,0:T(8,128)} fusion(f32[64,128,256]{2,1,0:T(8,128)} %get-tuple-element.287, s32[32]{0:T(128)S(1)} %get-tuple-element.252, f32[32,128,256]{2,1,0:T(8,128)} %fusion.48), kind=kCustom, calls=%fused_computation.3.clone.1 | custom fusion | flops 1048576 | bytes 12583040 | tf_op jit(solution)/shard_map/while/body/eval_jaxpr/scatter-add | solution.py:41
  622.6 10.0 %scatter_fusion.1 = f32[64,128,256]{2,1,0:T(8,128)} fusion(f32[64,128,256]{2,1,0:T(8,128)} %get-tuple-element.287, s32[32]{0:T(128)S(1)} %get-tuple-element.252, f32[32,128,256]{2,1,0:T(8,128)} %fusion.48), kind=kCustom, calls=%fused_computation.3.clone.1 | custom fusion | flops 1048576 | bytes 12583040 | tf_op jit(solution)/shard_map/while/body/eval_jaxpr/scatter-add | solution.py:41
  641.4 10.1 %scatter_fusion.1 = f32[64,128,256]{2,1,0:T(8,128)} fusion(f32[64,128,256]{2,1,0:T(8,128)} %get-tuple-element.287, s32[32]{0:T(128)S(1)} %get-tuple-element.252, f32[32,128,256]{2,1,0:T(8,128)} %fusion.48), kind=kCustom, calls=%fused_computation.3.clone.1 | custom fusion | flops 1048576 | bytes 12583040 | tf_op jit(solution)/shard_map/while/body/eval_jaxpr/scatter-add | solution.py:41
  660.3 10.1 %scatter_fusion.1 = f32[64,128,256]{2,1,0:T(8,128)} fusion(f32[64,128,256]{2,1,0:T(8,128)} %get-tuple-element.287, s32[32]{0:T(128)S(1)} %get-tuple-element.252, f32[32,128,256]{2,1,0:T(8,128)} %fusion.48), kind=kCustom, calls=%fused_computation.3.clone.1 | custom fusion | flops 1048576 | bytes 12583040 | tf_op jit(solution)/shard_map/while/body/eval_jaxpr/scatter-add | solution.py:41
  679.1 10.1 %scatter_fusion.1 = f32[64,128,256]{2,1,0:T(8,128)} fusion(f32[64,128,256]{2,1,0:T(8,128)} %get-tuple-element.287, s32[32]{0:T(128)S(1)} %get-tuple-element.252, f32[32,128,256]{2,1,0:T(8,128)} %fusion.48), kind=kCustom, calls=%fused_computation.3.clone.1 | custom fusion | flops 1048576 | bytes 12583040 | tf_op jit(solution)/shard_map/while/body/eval_jaxpr/scatter-add | solution.py:41
  697.9 9.9 %scatter_fusion.1 = f32[64,128,256]{2,1,0:T(8,128)} fusion(f32[64,128,256]{2,1,0:T(8,128)} %get-tuple-element.287, s32[32]{0:T(128)S(1)} %get-tuple-element.252, f32[32,128,256]{2,1,0:T(8,128)} %fusion.48), kind=kCustom, calls=%fused_computation.3.clone.1 | custom fusion | flops 1048576 | bytes 12583040 | tf_op jit(solution)/shard_map/while/body/eval_jaxpr/scatter-add | solution.py:41
  716.6 9.9 %scatter_fusion.1 = f32[64,128,256]{2,1,0:T(8,128)} fusion(f32[64,128,256]{2,1,0:T(8,128)} %get-tuple-element.287, s32[32]{0:T(128)S(1)} %get-tuple-element.252, f32[32,128,256]{2,1,0:T(8,128)} %fusion.48), kind=kCustom, calls=%fused_computation.3.clone.1 | custom fusion | flops 1048576 | bytes 12583040 | tf_op jit(solution)/shard_map/while/body/eval_jaxpr/scatter-add | solution.py:41
  729.3 97.6 %reduce-scatter.5.cloned.1.call-done = f32[512,256]{1,0:T(8,128)} async-done(((f32[8192,256]{1,0:T(8,128)}), f32[512,256]{1,0:T(8,128)}) %reduce-scatter.5.cloned.1.call-update) | async-done | bytes 524304 | tf_op jit(solution)/shard_map/reduce_scatter | solution.py:47
  (151 shorter events, 157.1 us)
Async XLA Ops:
  7.2 319.2 %copy-start = (bf16[256,256]{1,0:T(8,128)(2,1)S(1)}, bf16[256,256]{1,0:T(8,128)(2,1)}, u32[]{:S(2)}) copy-start(bf16[256,256]{1,0:T(8,128)(2,1)} %param.15) | copy-start | bytes 393220
  7.2 45.7 %all-gather.3.cloned.1.call-start = ((), (), s32[]{:S(2)}) async-start(), calls=%async_computation.2 | async-start | bytes 4456448 | tf_op jit(solution)/shard_map/all_gather | solution.py:71
  7.9 317.2 %reduce-scatter.3.cloned.1.call-start = ((), (), s32[]{:S(2)}) async-start(), calls=%async_computation.3 | async-start | bytes 8912896 | tf_op jit(solution)/shard_map/reduce_scatter | solution.py:86
  204.0 0.7 copy-start.3
  204.0 1.0 copy-start.1
  204.0 1.0 copy-start.2
  204.0 122.4 %copy-start.4 = (bf16[512,256]{1,0:T(8,128)(2,1)S(1)}, bf16[512,256]{1,0:T(8,128)(2,1)}, u32[]{:S(2)}) copy-start(bf16[512,256]{1,0:T(8,128)(2,1)} %param.16) | copy-start | bytes 786436
  204.0 290.0 %all-reduce.5.cloned.1.call-start = ((), (), s32[]{:S(2)}) async-start(), calls=%async_computation.6 | async-start | bytes 1048576 | tf_op jit(solution)/shard_map/psum | solution.py:11
  329.4 242.7 %all-gather.5.cloned.1.call-start = ((), (), s32[]{:S(2)}) async-start(), calls=%async_computation.4 | async-start | bytes 4456448 | tf_op jit(solution)/shard_map/all_gather | solution.py:32
  330.5 396.1 %all-reduce.7.cloned.1.call-start = ((), (), s32[]{:S(2)}) async-start(), calls=%async_computation.7 | async-start | bytes 1048576 | tf_op jit(solution)/shard_map/psum | solution.py:12
  494.1 332.9 %reduce-scatter.5.cloned.1.call-start = ((), (), s32[]{:S(2)}) async-start(), calls=%async_computation.5 | async-start | bytes 8912896 | tf_op jit(solution)/shard_map/reduce_scatter | solution.py:47
Sparse Core Ops, SparseCore 0:
  9.9 42.9 all-gather.2
  204.1 120.9 reduce-scatter.2
  329.6 164.4 all-reduce.4
  497.2 74.8 all-gather.4
  574.8 122.3 all-reduce.6
  726.7 100.2 reduce-scatter.4
